TPU v7x, 32 devices: a whole 2x2x4 slice. The times are simulated.
32 devices in a mesh: row: 8 (over y, x, core), col: 4 (over z).
Axes of the slice: x: 2, y: 2, z: 4, core: 2. Of those that a mesh axis runs over, the one named last changes fastest.
Arguments:
- loads: float32 [3, 24576], P(None, 'row'), may hold values from -6 to 6
- nd_source: int32 [24576], P('row'), may hold values from 0 to 24575, as said below
- panel: bfloat16 [24576, 512], P('row', 'col'), as said below
- trailing: bfloat16 [24576, 24576], P('row', 'col'), may hold values from -6 to 6
- pattern: int32 [192, 192], P('row', 'col'), may hold values from 0 to 1
- owner: int32 [8], replicated, may hold values from 0 to 7, each once
Outputs:
- loads_out: float32 [3, 24576], P(None, 'row')
- trailing_out: bfloat16 [24576, 24576], P('row', 'col')
Inputs may be any that keep to these rules, and one draw needn't show every extreme that they name: `nd_source`: a permutation; the rows t * 3072 to (t + 1) * 3072 - 1 take, from each block s of 3072 columns, exactly the columns s * 3072 + t * 384 to s * 3072 + (t + 1) * 384 - 1. `panel`: the 512 x 512 block at rows owner[0] * 3072 has a positive definite symmetric part. `owner`: a permutation of the row indices.
All inputs are finite; a program needn't handle non-finite values.
Results may differ from a plain program's by a relative error of at most 0.005.
Values may be sent and summed in bfloat16 or wider, within the bound.
A program may use at most 256 MiB of HBM per device.

v0:
```python
import jax
import jax.numpy as jnp
from jax import lax
from jax.sharding import PartitionSpec as P


def broadcast(array, axis, root):
    mine = lax.axis_index(axis) == root
    return lax.psum(jnp.where(mine, array, jnp.zeros_like(array)), axis)


def per_device(loads, nd_source, panel, trailing, pattern, owner):
    row_dev = panel.shape[0]
    row_count = lax.axis_size("row")
    col_count = lax.axis_size("col")
    pivot_size = panel.shape[1] * col_count
    share_size = row_dev // row_count
    row_place = lax.axis_index("row")
    col_place = lax.axis_index("col")
    arrived = lax.all_to_all(loads, "row", split_axis=1, concat_axis=1, tiled=True)
    source_slot = nd_source // row_dev * share_size + (nd_source % row_dev - row_place * share_size)
    regrouped = jnp.take(arrived, source_slot, axis=1)
    panel_rows = lax.all_gather(panel, "col", axis=1, tiled=True)
    owner_row = owner[0]
    pivot_block, pivot_loads = (
        broadcast(
            panel_rows[:pivot_size].astype(jnp.float32).astype(jnp.bfloat16), "row", owner_row
        ).astype(jnp.float32),
        broadcast(regrouped[:, :pivot_size].astype(jnp.bfloat16), "row", owner_row).astype(
            jnp.float32
        ),
    )
    symmetric = 0.5 * (pivot_block + pivot_block.T)
    lower_factor = jnp.linalg.cholesky(symmetric)
    inverse = lax.linalg.triangular_solve(
        lower_factor, jnp.eye(pivot_size, dtype=jnp.float32), left_side=True, lower=True
    )
    inverse_half = inverse.astype(jnp.bfloat16)
    factor_rows = jnp.dot(panel_rows, inverse_half.T, preferred_element_type=jnp.float32).astype(
        jnp.bfloat16
    )
    pivot_solve = jnp.dot(inverse, pivot_loads.T, precision=lax.Precision.HIGHEST)
    update = jnp.dot(
        factor_rows.astype(jnp.float32), pivot_solve, precision=lax.Precision.HIGHEST
    ).T
    pivot_start = owner_row * row_dev
    positions = row_place * row_dev + jnp.arange(row_dev, dtype=jnp.int32)
    in_pivot = (positions >= pivot_start) & (positions < pivot_start + pivot_size)
    pivot_offset = jnp.clip(positions - pivot_start, 0, pivot_size - 1)
    loads_out = jnp.where(
        in_pivot[None, :], jnp.take(pivot_solve.T, pivot_offset, axis=1), regrouped - update
    )
    holders = row_count // col_count
    pieces = []
    for member in range(holders):
        pieces.append(broadcast(factor_rows, "row", col_place * holders + member))
    factor_cols = jnp.concatenate(pieces, axis=0)
    block_rows = pattern.shape[0]
    block_cols = pattern.shape[1]
    block_size = trailing.shape[0] // block_rows
    col_dev = trailing.shape[1]
    product = jnp.einsum("ik,jk->ij", factor_rows, factor_cols, preferred_element_type=jnp.float32)
    masked = (
        product.reshape(block_rows, block_size, block_cols, block_size)
        * pattern.astype(jnp.float32)[:, None, :, None]
    ).reshape(row_dev, col_dev)
    trailing_out = (trailing.astype(jnp.float32) - masked).astype(jnp.bfloat16)
    return (loads_out, trailing_out)


def solution(mesh):
    return jax.shard_map(
        per_device,
        mesh=mesh,
        in_specs=(P(None, "row"), P("row"), P("row", "col"), P("row", "col"), P("row", "col"), P()),
        out_specs=(P(None, "row"), P("row", "col")),
        check_vma=False,
    )
```

profile of v0, /device:TPU:0, one launch (start us, length us, event | category | flops | bytes accessed | tf_op | source)
XLA Modules:
  0.0 477.6 jit_solution(12243766047315229716)
XLA Ops:
  7.2 2.3 copy.22
  10.2 66.1 %all-gather.2.cloned.1.call-done = bf16[3072,512]{0,1:T(8,128)(2,1)} async-done(((bf16[3072,128]{0,1:T(8,128)(2,1)}), bf16[3072,512]{0,1:T(8,128)(2,1)}) %all-gather.2.cloned.1.call-update) | async-done | bytes 3145744 | tf_op jit(solution)/shard_map/all_gather | solution.py:23
  76.3 1.9 slice_select_fusion
  79.2 54.3 %all-reduce.5.cloned.1.call-done = bf16[512,512]{0,1:T(8,128)(2,1)} async-done(((bf16[512,512]{0,1:T(8,128)(2,1)}), bf16[512,512]{0,1:T(8,128)(2,1)}) %all-reduce.5.cloned.1.call-update) | async-done | bytes 524304 | tf_op jit(solution)/shard_map/psum | solution.py:9
  137.5 11.7 %cholesky.104 = f32[128,128]{1,0:T(8,128)S(1)} custom-call(f32[128,128]{1,0:T(8,128)S(1)} %cholesky.266), custom_call_target="Cholesky" | custom-call | tf_op jit(solution)/shard_map/jit(cholesky)/cholesky | solution.py:34
  149.2 9.8 %custom-call.30 = f32[1,128,128]{1,2,0:T(8,128)S(1)} custom-call(f32[1,128,128]{2,1,0:T(8,128)S(1)} %get-tuple-element.35), custom_call_target="InvertDiagBlocksLowerTriangular" | custom-call | tf_op jit(solution)/shard_map/jit(cholesky)/cholesky | solution.py:34
  161.7 11.7 %cholesky.217 = f32[128,128]{1,0:T(8,128)S(1)} custom-call(f32[128,128]{1,0:T(8,128)S(1)} %cholesky.270), custom_call_target="Cholesky" | custom-call | tf_op jit(solution)/shard_map/jit(cholesky)/cholesky | solution.py:34
  173.4 10.0 %custom-call.31 = f32[1,128,128]{1,2,0:T(8,128)S(1)} custom-call(f32[1,128,128]{2,1,0:T(8,128)S(1)} %get-tuple-element.32), custom_call_target="InvertDiagBlocksLowerTriangular" | custom-call | tf_op jit(solution)/shard_map/jit(cholesky)/cholesky | solution.py:34
  185.0 11.7 %cholesky.238 = f32[128,128]{1,0:T(8,128)S(1)} custom-call(f32[128,128]{1,0:T(8,128)S(1)} %cholesky.275), custom_call_target="Cholesky" | custom-call | tf_op jit(solution)/shard_map/jit(cholesky)/cholesky | solution.py:34
  197.3 9.8 %custom-call.32 = f32[1,128,128]{1,2,0:T(8,128)S(1)} custom-call(f32[1,128,128]{2,1,0:T(8,128)S(1)} %get-tuple-element.29), custom_call_target="InvertDiagBlocksLowerTriangular" | custom-call | tf_op jit(solution)/shard_map/jit(cholesky)/cholesky | solution.py:34
  208.6 11.9 %cholesky.255 = f32[128,128]{1,0:T(8,128)S(1)} custom-call(f32[128,128]{1,0:T(8,128)S(1)} %convolution_subtract_fusion.6), custom_call_target="Cholesky" | custom-call | tf_op jit(solution)/shard_map/jit(cholesky)/cholesky | solution.py:34
  224.5 7.6 %while.1 = (s32[]{:T(128)}, f32[512,512]{1,0:T(8,128)S(1)}, s32[4,2]{0,1:T(2,128)S(1)}, f32[4,128,128]{2,1,0:T(8,128)S(1)}, s32[]{:T(128)}) while((s32[]{:T(128)}, f32[512,512]{1,0:T(8,128)S(1)}, s32[4,2]{0,1:T(2,128)S(1)}, f32[4,128,128]{2,1,0:T(8,128)S(1)}, s32[]{:T(128)}) %tuple.34), condition=%wide.while_cond, body=%wide.while_body.sunk | while | flops 2 | bytes 131189 | solution.py:35
  225.1 1.3 bitcast_dynamic-update-slice_fusion.2
  227.0 1.3 bitcast_dynamic-update-slice_fusion.2
  228.9 1.3 bitcast_dynamic-update-slice_fusion.2
  230.8 1.3 bitcast_dynamic-update-slice_fusion.2
  232.1 39.3 %custom-call.33 = f32[4,128,128]{1,2,0:T(8,128)S(1)} custom-call(f32[4,128,128]{2,1,0:T(8,128)S(1)} %get-tuple-element.9), custom_call_target="InvertDiagBlocksLowerTriangular" | custom-call | tf_op jit(solution)/shard_map/triangular_solve | solution.py:35
  276.2 1.8 convolution_convert_fusion
  278.0 3.1 select_bitcast_fusion.1
  281.1 3.5 all-to-all-start
  284.8 5.1 %all-to-all-done = f32[3,8,384]{2,0,1:T(4,128)S(1)} async-done(((f32[3,8,384]{2,0,1:T(4,128)}), f32[3,8,384]{2,0,1:T(4,128)S(1)}, u32[]{:S(2)}, u32[]{:S(2)}) %all-to-all-start) | async-done | bytes 36896 | tf_op jit(solution)/shard_map/all_to_all | solution.py:20
  289.9 1.6 copy.25
  291.6 12.3 %gather_fusion = f32[3072,3]{1,0:T(8,128)} fusion(f32[3,3072]{0,1:T(8,128)} %bitcast.81, s32[3072]{0:T(1024)S(1)} %broadcast_clamp_fusion.1), kind=kCustom, calls=%fused_computation | custom fusion | bytes 86016 | tf_op jit(solution)/shard_map/jit(_take)/gather | solution.py:22
  303.8 1.9 copy.26
  305.8 12.4 %psum.29 = bf16[3,512]{1,0:T(4,128)(2,1)S(1)} all-reduce(bf16[3,512]{1,0:T(4,128)(2,1)S(1)} %fusion.49), channel_id=1, replica_groups=mesh['row'=8,'col'=4] {'row'}, use_global_device_ids=true, to_apply=%region_9.10 | all-reduce | flops 1536 | bytes 6144 | tf_op jit(solution)/shard_map/psum | solution.py:9
  318.2 1.7 fusion.14
  320.1 10.8 %gather_fusion.1 = f32[3072,3]{1,0:T(8,128)} fusion(f32[3,512]{0,1:T(8,128)S(1)} %copy.27, s32[3072]{0:T(1024)S(1)} %broadcast_clamp_fusion), kind=kCustom, calls=%fused_computation.1 | custom fusion | bytes 86016 | tf_op jit(solution)/shard_map/jit(_take)/gather | solution.py:51
  330.9 1.9 copy.28
  332.7 2.0 fusion.5
  334.7 50.3 %all-reduce.7.cloned.1.call-done = (bf16[3072,512]{0,1:T(8,128)(2,1)}, bf16[3072,512]{0,1:T(8,128)(2,1)}) async-done(((bf16[3072,512]{0,1:T(8,128)(2,1)}, bf16[3072,512]{0,1:T(8,128)(2,1)}), (bf16[3072,512]{0,1:T(8,128)(2,1)}, bf16[3072,512]{0,1:T(8,128)(2,1)})) %all-reduce.7.cloned.1.call-update) | async-done | bytes 6291472 | tf_op jit(solution)/shard_map/psum | solution.py:9
  385.0 23.8 %mul.44 = f32[24,128,48,128]{3,2,1,0:T(8,128)} broadcast(f32[24,48]{1,0:T(8,128)S(1)} %convert_element_type.36), dimensions={0,2} | broadcast | bytes 75502080 | tf_op jit(solution)/shard_map/mul | solution.py:64
  408.8 61.8 %fusion.1 = bf16[3072,6144]{1,0:T(8,128)(2,1)} fusion(f32[384,8,48,128]{3,2,1,0:T(8,128)} %bitcast.25, bf16[3072,6144]{1,0:T(8,128)(2,1)} %param.9, bf16[512,3072]{1,0:T(8,128)(2,1)S(1)} %convolution_convert_fusion, bf16[3072,512]{0,1:T(8,128)(2,1)} %get-tuple-element.18, bf16[3072,512]{0,1:T(8,128)(2,1)} %get-tuple-element.19), kind=kOutput, calls=%fused_computation.6 | convolution fusion | flops 19415433216 | bytes 160432128 | tf_op jit(solution)/shard_map/ik,jk->ij/dot_general | solution.py:62
  (73 shorter events, 20.2 us)
Async XLA Ops:
  7.2 69.2 %all-gather.2.cloned.1.call-start = ((), (), s32[]{:S(2)}) async-start(), calls=%async_computation.1 | async-start | bytes 3932160 | tf_op jit(solution)/shard_map/all_gather | solution.py:23
  9.5 123.9 %all-reduce.5.cloned.1.call-start = ((), (), s32[]{:S(2)}) async-start(), calls=%async_computation.2 | async-start | bytes 1048576 | tf_op jit(solution)/shard_map/psum | solution.py:9
  78.2 306.8 %all-reduce.7.cloned.1.call-start = ((), (), s32[]{:S(2)}) async-start(), calls=%async_computation.3 | async-start | bytes 12582912 | tf_op jit(solution)/shard_map/psum | solution.py:9
  136.5 1.0 copy-start
  271.4 4.7 copy-start.4
  273.5 1.9 copy-start.1
  274.4 1.1 copy-start.2
  275.5 0.7 copy-start.3
  281.1 3.5 copy-start.7
  281.1 3.6 copy-start.5
  281.1 3.7 copy-start.6
  281.1 8.8 %all-to-all-start = ((f32[3,8,384]{2,0,1:T(4,128)}), f32[3,8,384]{2,0,1:T(4,128)S(1)}, u32[]{:S(2)}, u32[]{:S(2)}) async-start(f32[3,8,384]{2,0,1:T(4,128)} %bitcast.13), calls=%async_computation | async-start | bytes 98304 | tf_op jit(solution)/shard_map/all_to_all | solution.py:20
Sparse Core Ops, SparseCore 0:
  10.1 66.1 all-gather.1
  80.0 53.4 all-reduce.4
  281.3 103.6 all-reduce.6
where the time goes:
time: 487 us; the launch traced here: 478 us
  waiting for transfers between devices  176 us (36%)
  other arithmetic  126 us (26%)
  matrix products  76.6 us (16%)
  local copies, waits for them, and re-layouts  65.7 us (13%)
  between operations  17.8 us (4%)
  blocking collectives  12.4 us (3%)
    psum x2, waiting for transfers between devices, broadcast(): return lax.psum(jnp.where(mine, array, jnp.zeros_like(array)), axis)  105 us
    another operation x14, other arithmetic, per_device(): lower_factor = jnp.linalg.cholesky(symmetric)  78.7 us
    all_gather x1, waiting for transfers between devices, per_device(): panel_rows = lax.all_gather(panel, 'col', axis=1, tiled=True)  66.1 us
    dot_general x1, matrix products, per_device(): jnp.einsum('ik,jk->ij', factor_rows, factor_cols, preferred_element_type=...  61.8 us
    another operation x3, other arithmetic, per_device(): lax.linalg.triangular_solve(lower_factor, jnp.eye(pivot_size, dtype=jnp.f...  39.4 us
    mul x1, local copies, waits for them, and re-layouts, per_device(): product.reshape(block_rows, block_size, block_cols, block_size)  23.8 us
    gather x2, local copies, waits for them, and re-layouts, per_device(): regrouped = jnp.take(arrived, source_slot, axis=1)  14.2 us
    gather x2, local copies, waits for them, and re-layouts, per_device(): jnp.take(pivot_solve.T, pivot_offset, axis=1)  12.7 us
  transfers between devices with their start and end apart: 4, of which 4 were waited for; matrix products, arithmetic and copies ran while one was open for 7% of the time, Pallas kernels for 0%

commit v1 on v0

v1 whole, which is shorter than its diff:
```python
import functools

import jax
import jax.numpy as jnp
from jax import lax
from jax.experimental import pallas as pl
from jax.experimental.pallas import tpu as pltpu
from jax.sharding import PartitionSpec as P

HIGHEST = lax.Precision.HIGHEST


def dot_nt(a, b, **kw):
    return lax.dot_general(a, b, (((1,), (1,)), ((), ())), preferred_element_type=jnp.float32, **kw)


def dot_nn(a, b, **kw):
    return lax.dot_general(a, b, (((1,), (0,)), ((), ())), preferred_element_type=jnp.float32, **kw)


def invert_block(d):
    nb = d.shape[0]
    rows = lax.broadcasted_iota(jnp.int32, (nb, nb), 0)
    cols = lax.broadcasted_iota(jnp.int32, (nb, nb), 1)
    w = (rows == cols).astype(jnp.float32)
    row_id = lax.broadcasted_iota(jnp.int32, (8, 1), 0)
    groups = nb // 8
    ds = [d[8 * g : 8 * g + 8] for g in range(groups)]
    ws = [w[8 * g : 8 * g + 8] for g in range(groups)]
    diag = (lax.broadcasted_iota(jnp.int32, (8, nb), 1), lax.broadcasted_iota(jnp.int32, (8, nb), 0))
    for k in range(nb - 1):
        g0 = k // 8
        row = ds[g0][k % 8 : k % 8 + 1]
        w_row = ws[g0][k % 8 : k % 8 + 1]
        inv = 1.0 / row[:, k : k + 1]
        row = row * inv
        w_row = w_row * inv
        for g in range(g0, groups):
            col = ds[g][:, k : k + 1]
            if g == g0:
                if k % 8 == 7:
                    continue
                col = jnp.where(row_id > k % 8, col, 0.0)
            ds[g] = ds[g] - col * row
            ws[g] = ws[g] - col * w_row
    out = []
    for g in range(groups):
        pivot = jnp.sum(jnp.where(diag[0] == diag[1] + 8 * g, ds[g], 0.0), axis=1, keepdims=True)
        out.append(ws[g] * lax.rsqrt(pivot))
    return jnp.concatenate(out, axis=0)


def factor_kernel(first, last, nb, a_in, w_in, a_ref, w_ref):
    n = a_in.shape[0]
    a_ref[...] = a_in[...]
    w_ref[...] = w_in[...]
    row_id = lax.broadcasted_iota(jnp.int32, (n, 1), 0)

    @pl.loop(first, last)
    def _(j):
        start = pl.multiple_of(j * nb, nb)
        here = pl.ds(start, nb)
        x = invert_block(a_ref[here, here])
        below = jnp.where(row_id >= start + nb, dot_nt(a_ref[:, here], x, precision=HIGHEST), 0.0)
        w_here = dot_nn(x, w_ref[here, :], precision=HIGHEST)
        w_ref[...] = w_ref[...] - dot_nn(below, w_here, precision=HIGHEST)
        w_ref[here, :] = w_here
        a_ref[...] = a_ref[...] - dot_nt(below, below, precision=HIGHEST)


def eliminate(a, w, first, last, nb):
    n = a.shape[0]
    shape = jax.ShapeDtypeStruct((n, n), jnp.float32)
    return pl.pallas_call(
        functools.partial(factor_kernel, first, last, nb),
        out_shape=(shape, shape),
        in_specs=[pl.BlockSpec(memory_space=pltpu.VMEM)] * 2,
        out_specs=[pl.BlockSpec(memory_space=pltpu.VMEM)] * 2,
        cost_estimate=pl.CostEstimate(flops=20_000_000_000, bytes_accessed=4 * n * n * 4, transcendentals=0),
        name="eliminate",
    )(a, w)


def trailing_kernel(block, chunk, flags, rows_ref, cols_ref, mask_ref, old_ref, new_ref):
    step = pl.program_id(0)
    tile, width = old_ref.shape
    for i in range(tile // block):
        here = pl.ds(i * block, block)
        block_row = step * (tile // block) + i

        @pl.loop(0, width // chunk)
        def _(j):
            there = pl.ds(pl.multiple_of(j * chunk, chunk), chunk)
            live = flags[block_row, j] != 0

            @pl.when(live)
            def _():
                product = dot_nt(rows_ref[here, :], cols_ref[there, :])
                mask = mask_ref[0, i : i + 1, there]
                new_ref[here, there] = (old_ref[here, there].astype(jnp.float32) - product * mask).astype(
                    new_ref.dtype
                )

            @pl.when(jnp.logical_not(live))
            def _():
                new_ref[here, there] = old_ref[here, there]


def update_trailing(trailing, factor_rows, factor_cols, pattern):
    height, width = trailing.shape
    depth = factor_rows.shape[1]
    block_rows, block_cols = pattern.shape
    block = height // block_rows
    per_tile = 2 if block_rows % 2 == 0 else 1
    tile = per_tile * block
    per_chunk = 8 if block_cols % 8 == 0 else 1
    chunk = per_chunk * block
    flags = jnp.max(pattern.reshape(block_rows, block_cols // per_chunk, per_chunk), axis=2)
    mask = jnp.broadcast_to(
        pattern.astype(jnp.float32)[:, :, None], (block_rows, block_cols, width // block_cols)
    ).reshape(block_rows // per_tile, per_tile, width)
    grid_spec = pltpu.PrefetchScalarGridSpec(
        num_scalar_prefetch=1,
        grid=(height // tile,),
        in_specs=[
            pl.BlockSpec((tile, depth), lambda i, f: (i, 0)),
            pl.BlockSpec((width, depth), lambda i, f: (0, 0), pipeline_mode=pl.Buffered(1)),
            pl.BlockSpec((1, per_tile, width), lambda i, f: (i, 0, 0)),
            pl.BlockSpec((tile, width), lambda i, f: (i, 0)),
        ],
        out_specs=pl.BlockSpec((tile, width), lambda i, f: (i, 0)),
    )
    return pl.pallas_call(
        functools.partial(trailing_kernel, block, chunk),
        grid_spec=grid_spec,
        out_shape=jax.ShapeDtypeStruct(trailing.shape, trailing.dtype),
        compiler_params=pltpu.CompilerParams(
            dimension_semantics=("arbitrary",), vmem_limit_bytes=40 * 1024 * 1024
        ),
        name="trailing",
    )(flags, factor_rows, factor_cols, mask, trailing)


def swap_add(array, axis):
    size = lax.axis_size(axis)
    bit = 1
    while bit < size:
        array = array + lax.ppermute(array, axis, [(i, i ^ bit) for i in range(size)])
        bit *= 2
    return array


def gather_columns(piece, axis):
    size = lax.axis_size(axis)
    me = lax.axis_index(axis)
    rows, width = piece.shape
    got = [piece]
    for shift in range(1, size):
        got.append(lax.ppermute(piece, axis, [(i, i ^ shift) for i in range(size)]))
    whole = jnp.zeros((rows, width * size), piece.dtype)
    for shift in range(size):
        whole = lax.dynamic_update_slice(whole, got[shift], (0, (me ^ shift) * width))
    return whole


def spread(panel_rows):
    row_count = lax.axis_size("row")
    col_count = lax.axis_size("col")
    holders = row_count // col_count
    group = lax.axis_index("row") // holders
    member = lax.axis_index("row") % holders
    away = group ^ lax.axis_index("col")
    bits = []
    bit = 1
    while bit < col_count:
        bits.append(bit)
        bit *= 2
    orders = [[bits[(m + t) % len(bits)] for t in range(len(bits))] for m in range(holders)]
    held = panel_rows
    for step in range(len(bits)):
        pairs = []
        takes = jnp.zeros((), jnp.bool_)
        for m in range(holders):
            span = sum(orders[m][:step])
            new = orders[m][step]
            for c in range(col_count):
                for q in range(col_count):
                    if (q ^ c) & ~span == 0:
                        source = (q * holders + m) * col_count + c
                        target = ((q ^ new) * holders + m) * col_count + c
                        pairs.append((source, target))
            takes = takes | ((member == m) & ((away & ~span) == new))
        came = lax.ppermute(held, ("row", "col"), pairs)
        held = jnp.where(takes, came, held)
    got = [held]
    for k in range(1, holders):
        got.append(lax.ppermute(held, "row", [(i, i ^ k) for i in range(row_count)]))
    pieces = []
    for j in range(holders):
        piece = got[0]
        for k in range(1, holders):
            piece = jnp.where((member ^ k) == j, got[k], piece)
        pieces.append(piece)
    return pieces


def per_device(loads, nd_source, panel, trailing, pattern, owner):
    row_dev = panel.shape[0]
    row_count = lax.axis_size("row")
    col_count = lax.axis_size("col")
    pivot_size = panel.shape[1] * col_count
    share_size = row_dev // row_count
    row_place = lax.axis_index("row")
    owner_row = owner[0]
    mine = row_place == owner_row

    piece = swap_add(jnp.where(mine, panel[:pivot_size], jnp.zeros((), panel.dtype)), "row")
    pivot_block = gather_columns(piece, "col").astype(jnp.float32)
    symmetric = 0.5 * (pivot_block + pivot_block.T)

    panel_rows = lax.all_gather(panel, "col", axis=1, tiled=True)

    nb = min(128, pivot_size)
    blocks = pivot_size // nb
    a, w = eliminate(symmetric, jnp.eye(pivot_size, dtype=jnp.float32), 0, blocks // 2, nb)
    a, w = eliminate(a, w, blocks // 2, blocks, nb)
    inverse = w
    inverse_half = inverse.astype(jnp.bfloat16)

    pieces = spread(panel_rows)

    arrived = lax.all_to_all(loads, "row", split_axis=1, concat_axis=1, tiled=True)
    source_slot = nd_source // row_dev * share_size + (nd_source % row_dev - row_place * share_size)
    regrouped = jnp.take(arrived, source_slot, axis=1)
    pivot_loads = lax.psum(jnp.where(mine, regrouped[:, :pivot_size], 0.0), "row")

    factor_rows = dot_nt(panel_rows, inverse_half).astype(jnp.bfloat16)
    pivot_solve = dot_nt(pivot_loads, inverse, precision=HIGHEST)
    update = dot_nt(pivot_solve, factor_rows.astype(jnp.float32), precision=HIGHEST)
    plain = regrouped - update
    head = jnp.where(mine, pivot_solve, plain[:, :pivot_size])
    loads_out = jnp.concatenate([head, plain[:, pivot_size:]], axis=1)

    factor_cols = jnp.concatenate(
        [dot_nt(piece, inverse_half).astype(jnp.bfloat16) for piece in pieces], axis=0
    )
    trailing_out = update_trailing(trailing, factor_rows, factor_cols, pattern)
    return (loads_out, trailing_out)


def solution(mesh):
    return jax.shard_map(
        per_device,
        mesh=mesh,
        in_specs=(P(None, "row"), P("row"), P("row", "col"), P("row", "col"), P("row", "col"), P()),
        out_specs=(P(None, "row"), P("row", "col")),
        check_vma=False,
    )
```

time: 487 us -> 328 us (0.67)
  the two profiles are of different devices: /device:TPU:0 before, /device:TPU:1 now
where the time goes in v1:
time: 328 us; the launch traced here: 327 us
  Pallas kernels  105 us (32%)
  waiting for transfers between devices  93.3 us (28%)
  blocking collectives  38.3 us (12%)
  starting transfers between devices  25.7 us (8%)
  matrix products  19.6 us (6%)
  local copies, waits for them, and re-layouts  15.3 us (5%)
  between operations  15 us (5%)
  other arithmetic  14.9 us (5%)
    all_gather x1, waiting for transfers between devices, per_device(): panel_rows = lax.all_gather(panel, 'col', axis=1, tiled=True)  65.6 us
    pallas_call x2, Pallas kernels, eliminate(): pl.pallas_call(functools.partial(factor_kernel, first, last, nb), out_sha...  57.7 us
    pallas_call x1, Pallas kernels, update_trailing(): pl.pallas_call(functools.partial(trailing_kernel, block, chunk), grid_spe...  47 us
    psum x1, blocking collectives, per_device(): lax.psum(jnp.where(mine, regrouped[:, :pivot_size], 0.0), 'row')  38.3 us
    all_to_all x1, waiting for transfers between devices, per_device(): lax.all_to_all(loads, 'row', split_axis=1, concat_axis=1, tiled=True)  22.5 us
    dot_general x5, matrix products, dot_nt(): lax.dot_general(a, b, (((1,), (1,)), ((), ())), preferred_element_type=jn...  19.6 us
    ppermute x2, starting transfers between devices, spread(): came = lax.ppermute(held, ('row', 'col'), pairs)  13.1 us
    gather x2, local copies, waits for them, and re-layouts, per_device(): regrouped = jnp.take(arrived, source_slot, axis=1)  12.8 us
  transfers between devices with their start and end apart: 11, of which 4 were waited for; matrix products, arithmetic and copies ran while one was open for 10% of the time, Pallas kernels for 18%

profile of v1, /device:TPU:1, one launch (start us, length us, event | category | flops | bytes accessed | tf_op | source)
XLA Modules:
  0.0 326.7 jit_solution(6384134145160596028)
XLA Ops:
  7.2 0.7 all-gather.2.cloned.1.call-update
  7.9 65.6 %all-gather.2.cloned.1.call-done = bf16[3072,512]{1,0:T(8,128)(2,1)} async-done(((bf16[3072,128]{1,0:T(8,128)(2,1)}), bf16[3072,512]{1,0:T(8,128)(2,1)}) %all-gather.2.cloned.1.call-update) | async-done | bytes 3145744 | tf_op jit(solution)/shard_map/all_gather | solution.py:221
  73.5 6.3 %collective-permute-start.6 = (bf16[3072,512]{1,0:T(8,128)(2,1)}, bf16[3072,512]{1,0:T(8,128)(2,1)}, u32[]{:S(2)}, u32[]{:S(2)}) collective-permute-start(bf16[3072,512]{1,0:T(8,128)(2,1)} %all-gather.2.cloned.1.call-done), channel_id=1, source_target_pairs={{0,8},{9,1},{18,26},{27,19},{4,20},{13,29},{22,6},{31,15}} | collective-permute-start | bytes 9437192 | tf_op jit(solution)/shard_map/ppermute | solution.py:193
  79.8 4.1 %all-to-all-start = ((f32[3,8,384]{2,0,1:T(4,128)}), f32[3,8,384]{2,0,1:T(4,128)S(1)}, u32[]{:S(2)}, u32[]{:S(2)}) async-start(f32[3,8,384]{2,0,1:T(4,128)} %bitcast.20), calls=%async_computation | async-start | bytes 98304 | tf_op jit(solution)/shard_map/all_to_all | solution.py:232
  84.0 0.9 slice.17
  85.9 0.7 compare_and_fusion
  87.1 1.5 collective-permute-start.1
  88.6 1.2 fusion.5.w_in
  90.6 22.5 %all-to-all-done = f32[3,8,384]{2,0,1:T(4,128)S(1)} async-done(((f32[3,8,384]{2,0,1:T(4,128)}), f32[3,8,384]{2,0,1:T(4,128)S(1)}, u32[]{:S(2)}, u32[]{:S(2)}) %all-to-all-start) | async-done | bytes 36896 | tf_op jit(solution)/shard_map/all_to_all | solution.py:232
  113.1 0.5 copy.19
  113.6 10.9 %gather_fusion = f32[3072,3]{1,0:T(8,128)} fusion(f32[3,3072]{0,1:T(8,128)S(1)} %bitcast.19, s32[3072]{0:T(1024)S(1)} %broadcast_clamp_fusion), kind=kCustom, calls=%fused_computation | custom fusion | bytes 86016 | tf_op jit(solution)/shard_map/jit(_take)/gather | solution.py:234
  124.5 1.9 copy.20
  126.5 2.2 collective-permute-start.2
  128.7 3.9 %broadcast_select_fusion = bf16[3072,512]{1,0:T(8,128)(2,1)} fusion(bf16[3072,512]{1,0:T(8,128)(2,1)} %collective-permute-done.6, bf16[3072,512]{1,0:T(8,128)(2,1)} %all-gather.2.cloned.1.call-done, pred[]{:T(512)S(6)} %or.7), kind=kLoop, calls=%fused_computation.9 | loop fusion | flops 1572864 | bytes 9437185 | tf_op jit(solution)/shard_map/jit(_where)/select_n | solution.py:194
  132.6 6.8 %collective-permute-start.7 = (bf16[3072,512]{1,0:T(8,128)(2,1)}, bf16[3072,512]{1,0:T(8,128)(2,1)}, u32[]{:S(2)}, u32[]{:S(2)}) collective-permute-start(bf16[3072,512]{1,0:T(8,128)(2,1)} %broadcast_select_fusion), channel_id=1, source_target_pairs={{0,16},{8,24},{1,17},{9,25},{18,2},{26,10},{19,3},{27,11},{4,12},{... | collective-permute-start | bytes 9437192 | tf_op jit(solution)/shard_map/ppermute | solution.py:193
  139.5 0.7 collective-permute-start.4
  140.2 38.3 %psum.7 = f32[3,512]{1,0:T(4,128)S(1)} all-reduce(f32[3,512]{1,0:T(4,128)S(1)} %slice_select_fusion.1), channel_id=1, replica_groups=mesh['row'=8,'col'=4] {'row'}, use_global_device_ids=true, to_apply=%region_0.1 | all-reduce | flops 1536 | bytes 12288 | tf_op jit(solution)/shard_map/psum | solution.py:235
  178.5 2.8 collective-permute-start.5
  181.4 4.0 %collective-permute-done.5 = bf16[512,128]{0,1:T(8,128)(2,1)S(1)} collective-permute-done((bf16[512,128]{0,1:T(8,128)(2,1)S(1)}, bf16[512,128]{0,1:T(8,128)(2,1)S(1)}, u32[]{:S(2)}, u32[]{:S(2)}) %collective-permute-start.5) | collective-permute-done | bytes 131104 | tf_op jit(solution)/shard_map/ppermute | solution.py:159
  185.6 1.1 fusion.4.a_in
  186.7 28.7 %eliminate.2 = (f32[512,512]{1,0:T(8,128)}, f32[512,512]{1,0:T(8,128)}) custom-call(f32[512,512]{1,0:T(8,128)} %fusion.4.a_in, f32[512,512]{1,0:T(8,128)} %fusion.5.w_in), custom_call_target="tpu_custom_call" | custom-call | flops 20000000000 | bytes 4194304 | tf_op jit(solution)/shard_map/eliminate/pallas_call | solution.py:74
  215.4 3.9 %broadcast_select_fusion.1 = bf16[3072,512]{1,0:T(8,128)(2,1)} fusion(bf16[3072,512]{1,0:T(8,128)(2,1)} %collective-permute-done.7, bf16[3072,512]{1,0:T(8,128)(2,1)} %broadcast_select_fusion, pred[]{:T(512)S(6)} %or.6), kind=kLoop, calls=%fused_computation.10 | loop fusion | flops 1572864 | bytes 9437185 | tf_op jit(solution)/shard_map/jit(_where)/select_n | solution.py:194
  219.3 1.1 collective-permute-start.8
  220.3 29.0 %eliminate.3 = (f32[512,512]{1,0:T(8,128)}, f32[512,512]{1,0:T(8,128)}) custom-call(f32[512,512]{1,0:T(8,128)} %get-tuple-element.5.a_in, f32[512,512]{1,0:T(8,128)} %get-tuple-element.6.w_in), custom_call_target="tpu_custom_call" | custom-call | flops 20000000000 | bytes 4194304 | tf_op jit(solution)/shard_map/eliminate/pallas_call | solution.py:74
  249.3 2.2 fusion.13
  251.5 4.1 %convolution_convert_fusion.2 = bf16[512,3072]{0,1:T(8,128)(2,1)S(1)} fusion(bf16[3072,512]{1,0:T(8,128)(2,1)} %all-gather.2.cloned.1.call-done, f32[512,512]{1,0:T(8,128)} %get-tuple-element.7), kind=kOutput, calls=%fused_computation.4 | convolution fusion | flops 1612447744 | bytes 7340032 | tf_op jit(solution)/shard_map/dot_general | solution.py:14
  255.6 2.5 convolution_subtract_fusion
  258.2 0.6 pad_maximum_fusion.1
  258.8 5.4 %convolution_convert_fusion = bf16[3072,512]{1,0:T(8,128)(2,1)} fusion(bf16[3072,512]{1,0:T(8,128)(2,1)} %collective-permute-done.8, bf16[3072,512]{1,0:T(8,128)(2,1)} %broadcast_select_fusion.1, pred[]{:T(512)S(6)} %eq.45, f32[512,512]{1,0:T(8,128)S(1)} %copy-done), kind=kOutput, calls=%fused_computation.2 | convolution fusion | flops 1614020608 | bytes 10485761 | tf_op jit(solution)/shard_map/dot_general | solution.py:14
  264.2 5.5 %convolution_convert_fusion.1 = bf16[3072,512]{1,0:T(8,128)(2,1)} fusion(bf16[3072,512]{1,0:T(8,128)(2,1)} %collective-permute-done.8, bf16[3072,512]{1,0:T(8,128)(2,1)} %broadcast_select_fusion.1, pred[]{:T(512)S(6)} %eq.38, f32[512,512]{1,0:T(8,128)S(1)} %copy-done), kind=kOutput, calls=%fused_computation.3 | convolution fusion | flops 1614020608 | bytes 10485761 | tf_op jit(solution)/shard_map/dot_general | solution.py:14
  269.6 3.3 pad_maximum_fusion.cols_ref
  272.9 47.0 %trailing.1 = bf16[3072,6144]{1,0:T(8,128)(2,1)} custom-call(s32[24,6]{1,0:T(8,128)S(1)} %copy.25.flags, bf16[3072,512]{1,0:T(8,128)(2,1)S(1)} %bitcast.18, bf16[6144,512]{1,0:T(8,128)(2,1)S(1)} %pad_maximum_fusion.cols_ref, f32[12,2,6144]{2,1,0:T(2,128)S(1)} %reshape.19.mask_ref, bf16[3072,6144]{1,0:T(8,128)(2,1)} %old_ref.1), custom_call_target="tpu_custom_call" | custom-call | tf_op jit(solution)/shard_map/trailing/pallas_call | solution.py:133
  (36 shorter events, 2.0 us)
Async XLA Ops:
  7.2 82.6 %copy-start.1 = (s32[24,48]{1,0:T(8,128)S(1)}, s32[24,48]{1,0:T(8,128)}, u32[]{:S(2)}) copy-start(s32[24,48]{1,0:T(8,128)} %param.10) | copy-start | bytes 13828
  7.2 66.3 %all-gather.2.cloned.1.call-start = ((), (), s32[]{:S(2)}) async-start(), calls=%async_computation.1 | async-start | bytes 3932160 | tf_op jit(solution)/shard_map/all_gather | solution.py:221
  73.5 55.2 %collective-permute-start.6 = (bf16[3072,512]{1,0:T(8,128)(2,1)}, bf16[3072,512]{1,0:T(8,128)(2,1)}, u32[]{:S(2)}, u32[]{:S(2)}) collective-permute-start(bf16[3072,512]{1,0:T(8,128)(2,1)} %all-gather.2.cloned.1.call-done), channel_id=1, source_target_pairs={{0,8},{9,1},{18,26},{27,19},{4,20},{13,29},{22,6},{31,15}} | collective-permute-start | bytes 9437192 | tf_op jit(solution)/shard_map/ppermute | solution.py:193
  79.8 33.3 %all-to-all-start = ((f32[3,8,384]{2,0,1:T(4,128)}), f32[3,8,384]{2,0,1:T(4,128)S(1)}, u32[]{:S(2)}, u32[]{:S(2)}) async-start(f32[3,8,384]{2,0,1:T(4,128)} %bitcast.20), calls=%async_computation | async-start | bytes 98304 | tf_op jit(solution)/shard_map/all_to_all | solution.py:232
  85.7 1.4 collective-permute-start
  87.1 39.3 %collective-permute-start.1 = (bf16[512,128]{0,1:T(8,128)(2,1)S(1)}, bf16[512,128]{0,1:T(8,128)(2,1)S(1)}, u32[]{:S(2)}, u32[]{:S(2)}) collective-permute-start(bf16[512,128]{0,1:T(8,128)(2,1)S(1)} %fusion.19), channel_id=1, source_target_pairs={{0,8},{4,12},{8,0},{12,4},{16,24},{20,28},{24,16},{28,20},{1,9},{5... | collective-permute-start | bytes 393224 | tf_op jit(solution)/shard_map/ppermute | solution.py:148
  126.5 12.9 %collective-permute-start.2 = (bf16[512,128]{0,1:T(8,128)(2,1)S(1)}, bf16[512,128]{0,1:T(8,128)(2,1)S(1)}, u32[]{:S(2)}, u32[]{:S(2)}) collective-permute-start(bf16[512,128]{0,1:T(8,128)(2,1)S(1)} %add.51), channel_id=1, source_target_pairs={{0,16},{4,20},{8,24},{12,28},{16,0},{20,4},{24,8},{28,12},{1,17},{... | collective-permute-start | bytes 393224 | tf_op jit(solution)/shard_map/ppermute | solution.py:148
  132.6 82.8 %collective-permute-start.7 = (bf16[3072,512]{1,0:T(8,128)(2,1)}, bf16[3072,512]{1,0:T(8,128)(2,1)}, u32[]{:S(2)}, u32[]{:S(2)}) collective-permute-start(bf16[3072,512]{1,0:T(8,128)(2,1)} %broadcast_select_fusion), channel_id=1, source_target_pairs={{0,16},{8,24},{1,17},{9,25},{18,2},{26,10},{19,3},{27,11},{4,12},{... | collective-permute-start | bytes 9437192 | tf_op jit(solution)/shard_map/ppermute | solution.py:193
  139.5 41.8 %collective-permute-start.4 = (bf16[512,128]{0,1:T(8,128)(2,1)S(1)}, bf16[512,128]{0,1:T(8,128)(2,1)S(1)}, u32[]{:S(2)}, u32[]{:S(2)}) collective-permute-start(bf16[512,128]{0,1:T(8,128)(2,1)S(1)} %get-tuple-element.9), channel_id=1, source_target_pairs={{0,2},{1,3},{2,0},{3,1},{4,6},{5,7},{6,4},{7,5},{8,10},{9,11},{10,... | collective-permute-start | bytes 393224 | tf_op jit(solution)/shard_map/ppermute | solution.py:159
  140.2 41.1 %collective-permute-start.3 = (bf16[512,128]{0,1:T(8,128)(2,1)S(1)}, bf16[512,128]{0,1:T(8,128)(2,1)S(1)}, u32[]{:S(2)}, u32[]{:S(2)}) collective-permute-start(bf16[512,128]{0,1:T(8,128)(2,1)S(1)} %get-tuple-element.9), channel_id=1, source_target_pairs={{0,1},{1,0},{2,3},{3,2},{4,5},{5,4},{6,7},{7,6},{8,9},{9,8},{10,11... | collective-permute-start | bytes 393224 | tf_op jit(solution)/shard_map/ppermute | solution.py:159
  178.5 6.8 %collective-permute-start.5 = (bf16[512,128]{0,1:T(8,128)(2,1)S(1)}, bf16[512,128]{0,1:T(8,128)(2,1)S(1)}, u32[]{:S(2)}, u32[]{:S(2)}) collective-permute-start(bf16[512,128]{0,1:T(8,128)(2,1)S(1)} %get-tuple-element.9), channel_id=1, source_target_pairs={{0,3},{1,2},{2,1},{3,0},{4,7},{5,6},{6,5},{7,4},{8,11},{9,10},{10,... | collective-permute-start | bytes 393224 | tf_op jit(solution)/shard_map/ppermute | solution.py:159
  219.3 39.5 %collective-permute-start.8 = (bf16[3072,512]{1,0:T(8,128)(2,1)}, bf16[3072,512]{1,0:T(8,128)(2,1)}, u32[]{:S(2)}, u32[]{:S(2)}) collective-permute-start(bf16[3072,512]{1,0:T(8,128)(2,1)} %broadcast_select_fusion.1), channel_id=1, source_target_pairs={{0,4},{4,0},{8,12},{12,8},{16,20},{20,16},{24,28},{28,24},{1,5},{5... | collective-permute-start | bytes 9437192 | tf_op jit(solution)/shard_map/ppermute | solution.py:197
  255.6 3.2 copy-start
Sparse Core Ops, SparseCore 0:
  9.5 63.9 all-gather.1
